TPU v7x, 32 devices: a whole 2x2x4 slice. The times are simulated.
32 devices in a mesh: grp: 2 (over x), tp: 8 (over z, y), section: 2 (over core).
Axes of the slice: x: 2, y: 2, z: 4, core: 2. Of those that a mesh axis runs over, the one named last changes fastest.
Arguments:
- hidden_in: bfloat16 [128, 4096], P(('grp', 'section')), parts along dimension 0, may hold values from -6 to 6
- temporal_gain: float32 [4096], replicated, may hold values from 0.5 to 1.5
- temporal_qkv: bfloat16 [3, 4096, 4096], P(None, None, 'tp'), may hold values from -0.09375 to 0.09375
- temporal_out_weight: bfloat16 [4096, 4096], P('tp'), may hold values from -0.125 to 0.125
- cache_keys: bfloat16 [128, 64, 4096], P(('grp', 'section'), None, 'tp'), parts along dimension 0, may hold values from -240 to 240
- cache_values: bfloat16 [128, 64, 4096], P(('grp', 'section'), None, 'tp'), parts along dimension 0, may hold values from -6 to 6
- lengths: int32 [128], P(('grp', 'section')), parts along dimension 0, may hold values from 1 to 64, as said below
- depth_in: bfloat16 [8, 4096, 1024], P('section', 'tp'), may hold values from -0.09375 to 0.09375
- depth_embed: bfloat16 [8, 2048, 1024], P('section', 'tp'), may hold values from -6 to 6
- depth_gain: float32 [1024], replicated, may hold values from 0.5 to 1.5
- depth_qkv: bfloat16 [8, 3, 1024, 1024], P('section', None, None, 'tp'), may hold values from -0.1875 to 0.1875
- depth_out_weight: bfloat16 [8, 1024, 1024], P('section', 'tp'), may hold values from -0.1875 to 0.1875
- head_gain: float32 [1024], replicated, may hold values from 0.5 to 1.5
- head_weight: bfloat16 [8, 1024, 2048], P('section', 'tp'), may hold values from -0.25 to 0.25
- tokens: int32 [128, 8], P('grp', 'section'), parts along dimension 0, may hold values from 0 to 2047
Outputs:
- temporal_out: bfloat16 [128, 4096], P(('grp', 'section'), 'tp'), parts along dimension 0
- logits: float32 [128, 8, 2048], P('grp', 'section', 'tp'), parts along dimension 0
There are 2 independent parts, one for each index of `grp`. A program takes and returns all parts, laid end to end along the dimension named above; an argument that names none is the same for every part. Nothing has to cross between parts.
Inputs may be any that keep to these rules, and one draw needn't show every extreme that they name: Cached positions 0 to lengths - 1 of a stream are live and the new token stands at position lengths; some stream of every group holds 64 live positions.
All inputs are finite; a program needn't handle non-finite values.
Results may differ from a plain program's by a relative error of at most 0.009.
Values may be sent and summed in bfloat16 or wider, within the bound.
A program may use at most 64 MiB of HBM per device.

v0:
```python
import functools
import math

import jax
import jax.numpy as jnp
from jax import lax
from jax.experimental import pallas as pl
from jax.experimental.pallas import tpu as pltpu
from jax.sharding import PartitionSpec as P

HEAD_DIM = 128
DEPTH_HDIM = 64


EPSILON = 1e-05


def passed_along(block, axis, distance):
    devices = range(lax.axis_size(axis))
    route = [(i - distance, i) for i in devices if i - distance in devices]
    return lax.ppermute(block, axis, route)


def from_partner(shard, axis, distance):
    return lax.ppermute(shard, axis, [(i, i ^ 1 << distance) for i in range(lax.axis_size(axis))])


def rms_norm(values, scale):
    wide = values.astype(jnp.float32)
    return wide * lax.rsqrt(jnp.mean(wide * wide, axis=-1, keepdims=True) + EPSILON) * scale


def rotate(vectors, positions):
    halfdim = vectors.shape[-1] // 2
    spacing = jnp.arange(halfdim, dtype=jnp.float32) / halfdim
    inverse = jnp.exp(-math.log(10000.0) * spacing)
    angles = positions.astype(jnp.float32)[:, None, None] * inverse[None, None, :]
    cosine = jnp.cos(angles)
    sine = jnp.sin(angles)
    first = vectors[..., :halfdim]
    second = vectors[..., halfdim:]
    return jnp.concatenate(
        [first * cosine - second * sine, first * sine + second * cosine], axis=-1
    )


def per_device(
    hidden_in,
    temporal_gain,
    temporal_qkv,
    temporal_out_weight,
    cache_keys,
    cache_values,
    lengths,
    depth_in,
    depth_embed,
    depth_gain,
    depth_qkv,
    depth_out_weight,
    head_gain,
    head_weight,
    tokens,
):
    local_streams = hidden_in.shape[0]
    local_cols = temporal_qkv.shape[2]
    local_heads = local_cols // HEAD_DIM
    cache_len = cache_keys.shape[1]
    normed = rms_norm(hidden_in, temporal_gain).astype(jnp.bfloat16)
    projected = jnp.einsum("sd,tdf->tsf", normed, temporal_qkv, preferred_element_type=jnp.float32)
    layout = (local_streams, local_heads, HEAD_DIM)
    queries = rotate(projected[0].reshape(layout), lengths).astype(jnp.bfloat16)
    keys_new = rotate(projected[1].reshape(layout), lengths).astype(jnp.bfloat16)
    values_new = projected[2].reshape(layout).astype(jnp.bfloat16)
    cached_keys = cache_keys.reshape(local_streams, cache_len, local_heads, HEAD_DIM)
    cached_values = cache_values.reshape(local_streams, cache_len, local_heads, HEAD_DIM)
    factor = 1.0 / math.sqrt(HEAD_DIM)
    scores = (
        jnp.einsum("shd,sphd->shp", queries, cached_keys, preferred_element_type=jnp.float32)
        * factor
    )
    own_score = (
        jnp.sum(queries.astype(jnp.float32) * keys_new.astype(jnp.float32), axis=-1) * factor
    )
    valid = jnp.arange(cache_len, dtype=jnp.int32)[None, None, :] < lengths[:, None, None]
    scores = jnp.where(valid, scores, -jnp.inf)
    highest = jnp.maximum(jnp.max(scores, axis=-1), own_score)
    expo = jnp.exp(scores - highest[..., None])
    own_expo = jnp.exp(own_score - highest)
    totals = jnp.sum(expo, axis=-1) + own_expo
    weights = (expo / totals[..., None]).astype(jnp.bfloat16)
    own_weight = (own_expo / totals).astype(jnp.bfloat16)
    mixed = jnp.einsum("shp,sphd->shd", weights, cached_values, preferred_element_type=jnp.float32)
    mixed = mixed + own_weight.astype(jnp.float32)[..., None] * values_new.astype(jnp.float32)
    mixed = mixed.astype(jnp.bfloat16).reshape(local_streams, local_cols)
    partial_rows = jnp.dot(mixed, temporal_out_weight, preferred_element_type=jnp.float32)
    summed = lax.psum_scatter(partial_rows, "tp", scatter_dimension=1, tiled=True)
    slice_width = summed.shape[1]
    tp_place = lax.axis_index("tp")
    resid_in = lax.dynamic_slice_in_dim(hidden_in, tp_place * slice_width, slice_width, 1)
    temporal = (resid_in.astype(jnp.float32) + summed).astype(jnp.bfloat16)
    all_rows = lax.all_gather(temporal, "section", axis=0, tiled=True)
    streams = all_rows.shape[0]
    codes = depth_in.shape[0]
    entry_part = jnp.einsum("sd,cde->sce", all_rows, depth_in, preferred_element_type=jnp.float32)
    vocab_local = depth_embed.shape[1]
    first_id = tp_place * vocab_local
    onehot = (
        tokens[:, :, None] == first_id + jnp.arange(vocab_local, dtype=jnp.int32)[None, None, :]
    ).astype(jnp.bfloat16)
    embedded = jnp.einsum("scv,cve->sce", onehot, depth_embed, preferred_element_type=jnp.float32)
    entry_terms = entry_part + embedded
    hidden_rows = head_weight.shape[1]
    hidden_start = tp_place * hidden_rows
    entry = lax.psum(entry_terms, "tp")
    depth_normed = rms_norm(entry, depth_gain).astype(jnp.bfloat16)
    dproj = jnp.einsum(
        "sce,ctef->tscf", depth_normed, depth_qkv, preferred_element_type=jnp.float32
    ).astype(jnp.bfloat16)
    prior_keys, prior_values = passed_along((dproj[1], dproj[2]), "section", 1)
    depth_cols = dproj.shape[3]
    head_part = min(depth_cols, DEPTH_HDIM)
    local_parts = depth_cols // head_part
    sharers = DEPTH_HDIM // head_part
    all_keys = jnp.concatenate([prior_keys, dproj[1]], axis=1).reshape(
        streams, 2 * codes, local_parts, head_part
    )
    all_values = jnp.concatenate([prior_values, dproj[2]], axis=1).reshape(
        streams, 2 * codes, local_parts, head_part
    )
    depth_queries = dproj[0].reshape(streams, codes, local_parts, head_part)
    depth_scores = jnp.einsum(
        "sqhd,skhd->shqk", depth_queries, all_keys, preferred_element_type=jnp.float32
    )
    for level in range(sharers.bit_length() - 1):
        depth_scores = depth_scores + from_partner(depth_scores, "tp", level)
    depth_scores = depth_scores * (1.0 / math.sqrt(DEPTH_HDIM))
    section_place = lax.axis_index("section")
    query_pos = jnp.arange(codes, dtype=jnp.int32)[:, None]
    key_pos = jnp.arange(2 * codes, dtype=jnp.int32)[None, :]
    allowed = jnp.where(key_pos < codes, section_place > 0, key_pos - codes <= query_pos)
    depth_scores = jnp.where(allowed[None, None], depth_scores, -jnp.inf)
    depth_top = jnp.max(depth_scores, axis=-1, keepdims=True)
    depth_expo = jnp.exp(depth_scores - depth_top)
    depth_weights = (depth_expo / jnp.sum(depth_expo, axis=-1, keepdims=True)).astype(jnp.bfloat16)
    depth_mixed = jnp.einsum(
        "shqk,skhd->sqhd", depth_weights, all_values, preferred_element_type=jnp.float32
    ).astype(jnp.bfloat16)
    depth_mixed = depth_mixed.reshape(streams, codes, depth_cols)
    depth_terms = jnp.einsum(
        "scf,cfe->sce", depth_mixed, depth_out_weight, preferred_element_type=jnp.float32
    )
    resid = entry + lax.psum(depth_terms, "tp")
    head_normed = rms_norm(resid, head_gain).astype(jnp.bfloat16)
    own_hidden = lax.dynamic_slice_in_dim(head_normed, hidden_start, hidden_rows, 2)
    partial_logits = jnp.einsum(
        "sce,cev->scv", own_hidden, head_weight, preferred_element_type=jnp.float32
    )
    logits = lax.psum_scatter(partial_logits, "tp", scatter_dimension=2, tiled=True)
    return (temporal, logits)


MESH = pl.DeviceIdType.MESH


def normalised(wide, scale):
    return wide * lax.rsqrt(jnp.mean(wide * wide, axis=-1, keepdims=True) + EPSILON) * scale


def product(left, right):
    return jnp.dot(left, right, preferred_element_type=jnp.float32)


def tick_kernel(
    n, pieces,
    hidden_ref, gain_ref, lens_ref, tokens_ref, dgain_ref, hgain_ref,
    qkv_hbm, keys_hbm, values_hbm, outw_hbm, din_hbm, emb_hbm, dqkv_hbm, dout_hbm, headw_hbm,
    temporal_ref, logits_ref,
    qkv, keys, values, outw, din, emb, dqkv, dout, headw,
    tbuf, rows, ent, ebuf, nrm, kvs, kvr, mix, dbuf, lbuf, squares,
    load_sem, send_sem, recv_sem, pair_send, pair_recv,
):
    me = lax.axis_index("tp")
    sec = lax.axis_index("section")
    s_local, width = hidden_ref.shape
    cols = qkv.shape[2]
    heads = cols // HEAD_DIM
    cache_len = keys.shape[1]
    codes = din.shape[0]
    streams = 2 * s_local
    total = codes * streams
    bf = jnp.bfloat16

    span = width // pieces
    loads = {}
    slot = 0

    def load(name, source, target):
        nonlocal slot
        loads[name] = pltpu.make_async_copy(source, target, load_sem.at[slot])
        loads[name].start()
        slot += 1

    for t in range(3):
        for k in range(pieces):
            part = pl.ds(k * span, span)
            load(("qkv", t, k), qkv_hbm.at[t, part, :], qkv.at[t, part, :])
    load("keys", keys_hbm, keys)
    load("values", values_hbm, values)
    load("outw", outw_hbm, outw)
    barrier = pltpu.get_barrier_semaphore()
    for d in range(1, n):
        pl.semaphore_signal(
            barrier, inc=1, device_id={"tp": lax.rem(me + d, n)}, device_id_type=MESH
        )
    pl.semaphore_signal(barrier, inc=1, device_id={"section": 1 - sec}, device_id_type=MESH)

    def to_peer(phase, d, source, target, peer):
        return pltpu.make_async_remote_copy(
            src_ref=source, dst_ref=target,
            send_sem=send_sem.at[phase, d], recv_sem=recv_sem.at[phase, d],
            device_id={"tp": peer}, device_id_type=MESH,
        )

    def to_partner(phase, source, target):
        return pltpu.make_async_remote_copy(
            src_ref=source, dst_ref=target,
            send_sem=pair_send.at[phase], recv_sem=pair_recv.at[phase],
            device_id={"section": 1 - sec}, device_id_type=MESH,
        )

    pending = []
    half_n = n // 2
    pair = lax.rem(me, 2)
    spot = me // 2
    mate = 2 * spot + 1 - pair
    order = sorted(range(1, half_n), key=lambda d: abs(d - half_n // 2))

    def halves(size):
        return [(h, slice(h * size // 2, (h + 1) * size // 2)) for h in range(2)]

    def summed_over_tp(phase, block_of, buf):
        firsts = []
        parts = halves(buf.shape[2])
        for i, d in enumerate(order + [0]):
            target = lax.rem(spot + d, half_n)
            buf[0, i] = block_of(2 * target + 1 - pair).astype(bf)
            for h, at in parts:
                firsts.append(
                    to_peer(2 * phase, 2 * i + h, buf.at[0, i, at], buf.at[1, i, at], mate)
                )
                firsts[-1].start()
        seconds = []
        for i, d in enumerate(order + [0]):
            target = lax.rem(spot + d, half_n)
            block = block_of(2 * target + pair)
            added = []
            for h, at in parts:
                firsts[2 * i + h].wait_recv()
                added.append(block[at] + buf[1, i, at].astype(jnp.float32))
                if d:
                    buf[2, i, at] = added[-1].astype(bf)
                    seconds.append(
                        to_peer(
                            2 * phase + 1, 2 * i + h, buf.at[2, i, at], buf.at[3, i, at],
                            2 * target + pair,
                        )
                    )
                    seconds[-1].start()
        pending.extend(firsts + seconds)
        return jnp.concatenate(added, axis=0), seconds

    def finished(block, seconds, buf):
        for i in range(half_n - 1):
            seconds[2 * i].wait_recv()
            seconds[2 * i + 1].wait_recv()
            block = block + buf[3, i].astype(jnp.float32)
        return block

    normed = normalised(hidden_ref[...].astype(jnp.float32), gain_ref[...]).astype(bf)
    half = HEAD_DIM // 2
    lane = lax.broadcasted_iota(jnp.int32, (s_local, HEAD_DIM), 1)
    spacing = lax.rem(lane, half).astype(jnp.float32) / half
    diagonal = lax.broadcasted_iota(jnp.int32, (s_local, s_local), 0) == lax.broadcasted_iota(
        jnp.int32, (s_local, s_local), 1
    )
    lens = jnp.sum(
        jnp.where(diagonal, lens_ref[...].astype(jnp.float32), 0.0), axis=1, keepdims=True
    )
    lens = jnp.broadcast_to(lens, (s_local, HEAD_DIM))
    angles = lens * jnp.exp(-math.log(10000.0) * spacing)
    cosine = jnp.cos(angles)
    sine = jnp.sin(angles)
    sine = jnp.where(lane < half, -sine, sine)
    proj = []
    for t in range(3):
        acc = None
        for k in range(pieces):
            loads["qkv", t, k].wait()
            term = product(normed[:, k * span:(k + 1) * span], qkv[t, k * span:(k + 1) * span, :])
            acc = term if acc is None else acc + term
        if t == 1:
            load("emb", emb_hbm, emb)
            load("din", din_hbm, din)
            load("dqkv", dqkv_hbm, dqkv)
            load("dout", dout_hbm, dout)
            load("headw", headw_hbm, headw)
        if t < 2:
            turned = []
            for h in range(heads):
                one = acc[:, h * HEAD_DIM:(h + 1) * HEAD_DIM]
                turned.append(one * cosine + pltpu.roll(one, half, 1) * sine)
            acc = jnp.concatenate(turned, axis=1)
        proj.append(acc.astype(bf).astype(jnp.float32))

    factor = 1.0 / math.sqrt(HEAD_DIM)
    loads["keys"].wait()
    loads["values"].wait()
    group = 8
    padded = 8
    owner = lax.broadcasted_iota(jnp.int32, (group, padded, cols), 2) // HEAD_DIM
    mine = owner == lax.broadcasted_iota(jnp.int32, (group, padded, cols), 1)
    place = lax.broadcasted_iota(jnp.int32, (group, padded, cache_len), 2).astype(jnp.float32)
    mixed = []
    for g in range(s_local // group):
        at = slice(g * group, (g + 1) * group)
        q_g = jnp.where(mine, proj[0][at][:, None, :], 0.0)
        scores = lax.dot_general(
            q_g.astype(bf), keys[at], (((2,), (2,)), ((0,), (0,))),
            preferred_element_type=jnp.float32,
        ) * factor
        own_score = jnp.sum(q_g * proj[1][at][:, None, :], axis=-1, keepdims=True) * factor
        live = place < lens[at, :cache_len][:, None, :]
        scores = jnp.where(live, scores, -jnp.inf)
        highest = jnp.maximum(jnp.max(scores, axis=-1, keepdims=True), own_score)
        expo = jnp.exp(scores - highest)
        own_expo = jnp.exp(own_score - highest)
        totals = jnp.sum(expo, axis=-1, keepdims=True) + own_expo
        weights = (expo / totals).astype(bf)
        own_weight = (own_expo / totals).astype(bf).astype(jnp.float32)
        out = lax.dot_general(
            weights, values[at], (((2,), (1,)), ((0,), (0,))),
            preferred_element_type=jnp.float32,
        )
        out = jnp.where(mine, out + own_weight * proj[2][at][:, None, :], 0.0)
        mixed.append(jnp.sum(out, axis=1))
    mixed = jnp.concatenate(mixed, axis=0).astype(bf)

    loads["outw"].wait()
    slim = width // n
    pl.semaphore_wait(barrier, n)

    def row_block(j):
        return product(mixed, outw[:, pl.ds(pl.multiple_of(j * slim, slim), slim)])

    summed, seconds = summed_over_tp(0, row_block, tbuf)

    vocab = emb.shape[1]
    loads["emb"].wait()
    ids = lax.broadcasted_iota(jnp.int32, (vocab, streams), 0) + me * vocab
    for c in range(codes):
        onehot = jnp.where(tokens_ref[c:c + 1, :] == ids, 1.0, 0.0).astype(bf)
        ent[c * streams:(c + 1) * streams, :] = lax.dot_general(
            onehot, emb[c], (((0,), (0,)), ((), ())), preferred_element_type=jnp.float32
        )
    loads["din"].wait()

    summed = finished(summed, seconds, tbuf)
    start = pl.multiple_of(me * slim, slim)
    temporal = (hidden_ref[:, pl.ds(start, slim)].astype(jnp.float32) + summed).astype(bf)
    temporal_ref[...] = temporal
    rows[sec] = temporal
    swap = to_partner(0, rows.at[sec], rows.at[sec])
    swap.start()
    pending.append(swap)
    swap.wait_recv()

    all_rows = rows[...].reshape(streams, slim)
    part = din.shape[2] // n

    def features(j):
        return pl.ds(pl.multiple_of(j * part, part), part)

    def entry_block(j):
        terms = [product(all_rows, din[c, :, features(j)]) for c in range(codes)]
        return ent[:, features(j)] + jnp.concatenate(terms, axis=0)

    def row_squares(block):
        return lax.dot_general(
            jnp.ones((8, part), jnp.float32), block * block, (((1,), (1,)), ((), ())),
            preferred_element_type=jnp.float32, precision=lax.Precision.HIGHEST,
        )

    def squares_out(which, phase, block):
        squares[which, me] = row_squares(block)
        sent = []
        for d in range(1, n):
            sent.append(
                to_peer(
                    phase, d, squares.at[which, me], squares.at[which, me], lax.rem(me + d, n)
                )
            )
            sent[-1].start()
        pending.extend(sent)
        return sent

    def row_factor(which, sent):
        for copy in sent:
            copy.wait_recv()
        mean = jnp.sum(squares[which], axis=0) / (n * part)
        column = lax.dot_general(
            mean, jnp.full((8, 128), 0.125, jnp.float32), (((0,), (0,)), ((), ())),
            preferred_element_type=jnp.float32, precision=lax.Precision.HIGHEST,
        )
        return lax.rsqrt(column + EPSILON)

    entry = finished(*summed_over_tp(1, entry_block, ebuf), ebuf)
    sent = squares_out(0, 8, entry)
    nrm[me] = (entry * dgain_ref[:, features(me)]).astype(bf)
    swaps = [to_peer(6, n - 1, nrm.at[me], nrm.at[me], mate)]
    swaps[0].start()
    copies = []
    parts = halves(nrm.shape[1])
    for i, d in enumerate(order):
        peer = 2 * lax.rem(spot + d, half_n) + pair
        for h, at in parts:
            copies.append(to_peer(6, 2 * i + h, nrm.at[me, at], nrm.at[me, at], peer))
            copies[-1].start()
    for i, d in enumerate(order):
        came = 2 * lax.rem(spot - d + half_n, half_n) + pair
        for h, at in parts:
            copies[2 * i + h].wait_recv()
            swaps.append(to_peer(7, 2 * i + h, nrm.at[came, at], nrm.at[came, at], mate))
            swaps[-1].start()
    pending += copies + swaps
    depth_factor = row_factor(0, sent)
    loads["dqkv"].wait()
    for copy in swaps:
        copy.wait_recv()

    lanes = dqkv.shape[3]
    queries = []
    for c in range(codes):
        at = slice(c * streams, (c + 1) * streams)
        x = jnp.concatenate([nrm[j, at, :] for j in range(n)], axis=1)
        r = depth_factor[at]
        queries.append((product(x, dqkv[c, 0]) * r).astype(bf).astype(jnp.float32))
        kvs[0, c] = (product(x, dqkv[c, 1]) * r).astype(bf)
        kvs[1, c] = (product(x, dqkv[c, 2]) * r).astype(bf)
    swap = to_partner(1, kvs, kvr)
    swap.start()
    pending.append(swap)
    row_head = lax.rem(lax.broadcasted_iota(jnp.int32, (2 * lanes, lanes), 0), lanes) // DEPTH_HDIM
    col_head = lax.broadcasted_iota(jnp.int32, (2 * lanes, lanes), 1) // DEPTH_HDIM
    ones = jnp.where(row_head == col_head, 1.0, 0.0).astype(bf)
    scale = 1.0 / math.sqrt(DEPTH_HDIM)

    def score(query, key):
        both = query * key.astype(jnp.float32)
        high = both.astype(bf)
        low = (both - high.astype(jnp.float32)).astype(bf)
        return product(jnp.concatenate([high, low], axis=1), ones) * scale

    local = [[score(queries[q], kvs[0, k]) for k in range(q + 1)] for q in range(codes)]
    swap.wait_recv()
    loads["dout"].wait()
    for q in range(codes):
        prior = [
            jnp.where(sec > 0, score(queries[q], kvr[0, k]), -jnp.inf) for k in range(codes)
        ]
        every = prior + local[q]
        top = every[0]
        for item in every[1:]:
            top = jnp.maximum(top, item)
        expo = [jnp.exp(item - top) for item in every]
        sums = expo[0]
        for item in expo[1:]:
            sums = sums + item
        out = None
        for k, item in enumerate(expo):
            value = kvr[1, k] if k < codes else kvs[1, k - codes]
            term = (item / sums).astype(bf).astype(jnp.float32) * value.astype(jnp.float32)
            out = term if out is None else out + term
        mix[q * streams:(q + 1) * streams, :] = out.astype(bf)

    def resid_block(j):
        return jnp.concatenate(
            [
                product(mix[c * streams:(c + 1) * streams, :], dout[c, :, features(j)])
                for c in range(codes)
            ],
            axis=0,
        )

    resid = entry + finished(*summed_over_tp(2, resid_block, dbuf), dbuf)
    hidden = (resid * hgain_ref[:, features(me)]).astype(bf)
    sent = squares_out(1, 9, resid)
    loads["headw"].wait()
    share = headw.shape[2] // n

    def vocab_block(j):
        there = pl.ds(pl.multiple_of(j * share, share), share)
        return jnp.concatenate(
            [product(hidden[c * streams:(c + 1) * streams, :], headw[c, :, there]) for c in range(codes)],
            axis=0,
        )

    out = finished(*summed_over_tp(5, vocab_block, lbuf), lbuf)
    out = out * row_factor(1, sent)[:, :1]
    logits_ref[...] = out.reshape(codes, streams, share)
    for copy in pending:
        copy.wait_send()


def fused(
    n, hidden_in, temporal_gain, temporal_qkv, temporal_out_weight, cache_keys, cache_values,
    lengths, depth_in, depth_embed, depth_gain, depth_qkv, depth_out_weight, head_gain,
    head_weight, tokens,
):
    s_local, width = hidden_in.shape
    codes, slim, deep = depth_in.shape
    streams = 2 * s_local
    total = codes * streams
    lanes = depth_qkv.shape[3]
    part = head_weight.shape[1]
    share = head_weight.shape[2] // n
    bf, f32 = jnp.bfloat16, jnp.float32
    pieces = 4
    big = [temporal_qkv, cache_keys, cache_values, temporal_out_weight, depth_in, depth_embed,
           depth_qkv, depth_out_weight, head_weight]
    vmem = pl.BlockSpec(memory_space=pltpu.VMEM)
    scratch = [pltpu.VMEM(a.shape, a.dtype) for a in big] + [
        pltpu.VMEM((4, n // 2, s_local, slim), bf),
        pltpu.VMEM((2, s_local, slim), bf),
        pltpu.VMEM((total, deep), f32),
        pltpu.VMEM((4, n // 2, total, part), bf),
        pltpu.VMEM((n, total, part), bf),
        pltpu.VMEM((2, codes, streams, lanes), bf),
        pltpu.VMEM((2, codes, streams, lanes), bf),
        pltpu.VMEM((total, lanes), bf),
        pltpu.VMEM((4, n // 2, total, part), bf),
        pltpu.VMEM((4, n // 2, total, share), bf),
        pltpu.VMEM((2, n, 8, total), f32),
        pltpu.SemaphoreType.DMA((3 * pieces + 8,)),
        pltpu.SemaphoreType.DMA((12, n)),
        pltpu.SemaphoreType.DMA((12, n)),
        pltpu.SemaphoreType.DMA((2,)),
        pltpu.SemaphoreType.DMA((2,)),
    ]
    temporal, logits = pl.pallas_call(
        functools.partial(tick_kernel, n, pieces),
        out_shape=(
            jax.ShapeDtypeStruct((s_local, slim), bf),
            jax.ShapeDtypeStruct((codes, streams, share), f32),
        ),
        in_specs=[vmem] * 6 + [pl.BlockSpec(memory_space=pl.ANY)] * 9,
        out_specs=(vmem, vmem),
        scratch_shapes=scratch,
        compiler_params=pltpu.CompilerParams(
            collective_id=0, has_side_effects=True, vmem_limit_bytes=60 * 1024 * 1024
        ),
    )(
        hidden_in, temporal_gain[None, :], lengths[None, :], tokens.T, depth_gain[None, :], head_gain[None, :],
        *big,
    )
    return temporal, jnp.swapaxes(logits, 0, 1)


def fits(n, arrays):
    hidden_in, depth_in, depth_qkv = arrays[0], arrays[7], arrays[10]
    total = depth_in.shape[0] * 2 * hidden_in.shape[0]
    return (
        lax.axis_size("section") == 2
        and n % 2 == 0
        and depth_qkv.shape[3] == 128
        and arrays[13].shape[1] % 128 == 0
        and arrays[13].shape[2] % (128 * n) == 0
        and total % (16 * n) == 0
        and hidden_in.shape[0] % 16 == 0
        and arrays[4].shape[1] <= HEAD_DIM
        and arrays[2].shape[2] <= 8 * HEAD_DIM
    )


def any_size(*arrays):
    n = lax.axis_size("tp")
    if fits(n, arrays):
        return fused(n, *arrays)
    return per_device(*arrays)


def solution(mesh):
    return jax.shard_map(
        any_size,
        mesh=mesh,
        in_specs=(
            P(("grp", "section"), None),
            P(),
            P(None, None, "tp"),
            P("tp", None),
            P(("grp", "section"), None, "tp"),
            P(("grp", "section"), None, "tp"),
            P(("grp", "section")),
            P("section", "tp", None),
            P("section", "tp", None),
            P(),
            P("section", None, None, "tp"),
            P("section", "tp", None),
            P(),
            P("section", "tp", None),
            P("grp", "section"),
        ),
        out_specs=(P(("grp", "section"), "tp"), P("grp", "section", "tp")),
        check_vma=False,
    )
```

profile of v0, /device:TPU:0, one launch (start us, length us, event | category | flops | bytes accessed | tf_op | source)
XLA Modules:
  0.0 80.1 jit_solution(8661471280146346251)
XLA Ops:
  0.6 76.3 %shard_map.158 = (bf16[32,512]{1,0:T(8,128)(2,1)}, f32[4,64,256]{2,1,0:T(8,128)}) custom-call(bf16[32,4096]{1,0:T(8,128)(2,1)} %hidden_ref.1, f32[1,4096]{1,0:T(1,128)} %bitcast.7, s32[1,32]{1,0:T(1,128)} %bitcast.11, s32[4,64]{1,0:T(4,128)} %bitcast.10, f32[1,1024]{1,0:T(1,128)} %bitcast.8, f32[1,1024]{1,0:T(1,128)} %bitcast.9, ...), custom_call_target="tpu_custom_call" | custom-call | tf_op jit(solution)/shard_map/pallas_call | solution.py:549
  76.9 1.8 %copy.17 = f32[64,4,256]{2,1,0:T(4,128)} copy(f32[64,4,256]{2,0,1:T(8,128)} %bitcast.6) | data formatting | bytes 524288
  78.7 1.4 %copy.19 = bf16[32,512]{1,0:T(8,128)(2,1)} copy(bf16[32,512]{1,0:T(8,128)(2,1)} %get-tuple-element.10) | data formatting | bytes 65536
where the time goes:
time: 80.3 us; the launch traced here: 80.1 us
  Pallas kernels  76.3 us (95%)
  local copies, waits for them, and re-layouts  3.2 us (4%)
    pallas_call x1, Pallas kernels, fused(): pl.pallas_call(functools.partial(tick_kernel, n, pieces), out_shape=(jax....  76.3 us
    unnamed x2, local copies, waits for them, and re-layouts  3.2 us

commit v1 on v0

--- a/solution.py
+++ b/solution.py
@@ -187,7 +187,6 @@
     cache_len = keys.shape[1]
     codes = din.shape[0]
     streams = 2 * s_local
-    total = codes * streams
     bf = jnp.bfloat16
 
     span = width // pieces
@@ -355,13 +354,16 @@
     summed, seconds = summed_over_tp(0, row_block, tbuf)
 
     vocab = emb.shape[1]
+    chunk_rows = codes * s_local
     loads["emb"].wait()
     ids = lax.broadcasted_iota(jnp.int32, (vocab, streams), 0) + me * vocab
     for c in range(codes):
         onehot = jnp.where(tokens_ref[c:c + 1, :] == ids, 1.0, 0.0).astype(bf)
-        ent[c * streams:(c + 1) * streams, :] = lax.dot_general(
+        looked_up = lax.dot_general(
             onehot, emb[c], (((0,), (0,)), ((), ())), preferred_element_type=jnp.float32
         )
+        for a in range(2):
+            ent[a, c * s_local:(c + 1) * s_local, :] = looked_up[a * s_local:(a + 1) * s_local]
     loads["din"].wait()
 
     summed = finished(summed, seconds, tbuf)
@@ -374,15 +376,58 @@
     pending.append(swap)
     swap.wait_recv()
 
-    all_rows = rows[...].reshape(streams, slim)
     part = din.shape[2] // n
+    share = headw.shape[2] // n
+    lanes = dqkv.shape[3]
+
+    def at_code(c):
+        return slice(c * s_local, (c + 1) * s_local)
 
     def features(j):
         return pl.ds(pl.multiple_of(j * part, part), part)
 
-    def entry_block(j):
-        terms = [product(all_rows, din[c, :, features(j)]) for c in range(codes)]
-        return ent[:, features(j)] + jnp.concatenate(terms, axis=0)
+    def first_sends(phase, a, block_of, buf):
+        sent = []
+        for i, d in enumerate(order + [0]):
+            target = lax.rem(spot + d, half_n)
+            buf[0, a, i] = block_of(2 * target + 1 - pair).astype(bf)
+            sent.append(
+                to_peer(2 * phase, 2 * i + a, buf.at[0, a, i], buf.at[1, a, i], mate)
+            )
+            sent[-1].start()
+        pending.extend(sent)
+        return sent
+
+    def second_sends(phase, a, block_of, buf, firsts):
+        sent = []
+        for i, d in enumerate(order + [0]):
+            target = lax.rem(spot + d, half_n)
+            block = block_of(2 * target + pair)
+            firsts[i].wait_recv()
+            block = block + buf[1, a, i].astype(jnp.float32)
+            if d:
+                buf[2, a, i] = block.astype(bf)
+                sent.append(
+                    to_peer(
+                        2 * phase + 1, 2 * i + a, buf.at[2, a, i], buf.at[3, a, i],
+                        2 * target + pair,
+                    )
+                )
+                sent[-1].start()
+        pending.extend(sent)
+        return block, sent
+
+    def gathered(a, block, sent, buf):
+        for i in range(half_n - 1):
+            sent[i].wait_recv()
+            block = block + buf[3, a, i].astype(jnp.float32)
+        return block
+
+    def entry_block(a):
+        def block_of(j):
+            terms = [product(rows[a], din[c, :, features(j)]) for c in range(codes)]
+            return ent[a, :, features(j)] + jnp.concatenate(terms, axis=0)
+        return block_of
 
     def row_squares(block):
         return lax.dot_general(
@@ -390,65 +435,65 @@
             preferred_element_type=jnp.float32, precision=lax.Precision.HIGHEST,
         )
 
-    def squares_out(which, phase, block):
-        squares[which, me] = row_squares(block)
+    def squares_out(which, a, block):
+        squares[which, a, me] = row_squares(block)
         sent = []
         for d in range(1, n):
             sent.append(
                 to_peer(
-                    phase, d, squares.at[which, me], squares.at[which, me], lax.rem(me + d, n)
+                    8 + which + 4 * a, d, squares.at[which, a, me], squares.at[which, a, me],
+                    lax.rem(me + d, n),
                 )
             )
             sent[-1].start()
         pending.extend(sent)
         return sent
 
-    def row_factor(which, sent):
+    def row_factor(which, a, sent):
         for copy in sent:
             copy.wait_recv()
-        mean = jnp.sum(squares[which], axis=0) / (n * part)
+        mean = jnp.sum(squares[which, a], axis=0) / (n * part)
         column = lax.dot_general(
             mean, jnp.full((8, 128), 0.125, jnp.float32), (((0,), (0,)), ((), ())),
             preferred_element_type=jnp.float32, precision=lax.Precision.HIGHEST,
         )
         return lax.rsqrt(column + EPSILON)
 
-    entry = finished(*summed_over_tp(1, entry_block, ebuf), ebuf)
-    sent = squares_out(0, 8, entry)
-    nrm[me] = (entry * dgain_ref[:, features(me)]).astype(bf)
-    swaps = [to_peer(6, n - 1, nrm.at[me], nrm.at[me], mate)]
-    swaps[0].start()
-    copies = []
-    parts = halves(nrm.shape[1])
-    for i, d in enumerate(order):
-        peer = 2 * lax.rem(spot + d, half_n) + pair
-        for h, at in parts:
-            copies.append(to_peer(6, 2 * i + h, nrm.at[me, at], nrm.at[me, at], peer))
+    def gather_sends(a, block):
+        nrm[me, a] = (block * dgain_ref[:, features(me)]).astype(bf)
+        copies = []
+        for i, d in enumerate(order):
+            peer = 2 * lax.rem(spot + d, half_n) + pair
+            copies.append(to_peer(6, 2 * i + a, nrm.at[me, a], nrm.at[me, a], peer))
             copies[-1].start()
-    for i, d in enumerate(order):
-        came = 2 * lax.rem(spot - d + half_n, half_n) + pair
-        for h, at in parts:
-            copies[2 * i + h].wait_recv()
-            swaps.append(to_peer(7, 2 * i + h, nrm.at[came, at], nrm.at[came, at], mate))
+        swaps = [to_peer(6, n - 2 + a, nrm.at[me, a], nrm.at[me, a], mate)]
+        swaps[0].start()
+        return copies, swaps
+
+    def gather_forwards(a, copies, swaps):
+        for i, d in enumerate(order):
+            came = 2 * lax.rem(spot - d + half_n, half_n) + pair
+            copies[i].wait_recv()
+            swaps.append(to_peer(7, 2 * i + a, nrm.at[came, a], nrm.at[came, a], mate))
             swaps[-1].start()
-    pending += copies + swaps
-    depth_factor = row_factor(0, sent)
-    loads["dqkv"].wait()
-    for copy in swaps:
-        copy.wait_recv()
-
-    lanes = dqkv.shape[3]
-    queries = []
-    for c in range(codes):
-        at = slice(c * streams, (c + 1) * streams)
-        x = jnp.concatenate([nrm[j, at, :] for j in range(n)], axis=1)
-        r = depth_factor[at]
-        queries.append((product(x, dqkv[c, 0]) * r).astype(bf).astype(jnp.float32))
-        kvs[0, c] = (product(x, dqkv[c, 1]) * r).astype(bf)
-        kvs[1, c] = (product(x, dqkv[c, 2]) * r).astype(bf)
-    swap = to_partner(1, kvs, kvr)
-    swap.start()
-    pending.append(swap)
+        pending.extend(copies + swaps)
+
+    def projections(a, swaps, sent):
+        r = row_factor(0, a, sent)
+        for copy in swaps:
+            copy.wait_recv()
+        queries = []
+        for c in range(codes):
+            x = jnp.concatenate([nrm[j, a, at_code(c), :] for j in range(n)], axis=1)
+            f = r[at_code(c)]
+            queries.append((product(x, dqkv[c, 0]) * f).astype(bf).astype(jnp.float32))
+            kvs[a, 0, c] = (product(x, dqkv[c, 1]) * f).astype(bf)
+            kvs[a, 1, c] = (product(x, dqkv[c, 2]) * f).astype(bf)
+        swap = to_partner(1 + a, kvs.at[a], kvr.at[a])
+        swap.start()
+        pending.append(swap)
+        return queries, swap
+
     row_head = lax.rem(lax.broadcasted_iota(jnp.int32, (2 * lanes, lanes), 0), lanes) // DEPTH_HDIM
     col_head = lax.broadcasted_iota(jnp.int32, (2 * lanes, lanes), 1) // DEPTH_HDIM
     ones = jnp.where(row_head == col_head, 1.0, 0.0).astype(bf)
@@ -460,53 +505,78 @@
         low = (both - high.astype(jnp.float32)).astype(bf)
         return product(jnp.concatenate([high, low], axis=1), ones) * scale
 
-    local = [[score(queries[q], kvs[0, k]) for k in range(q + 1)] for q in range(codes)]
-    swap.wait_recv()
+    def attention(a, queries, swap):
+        local = [[score(queries[q], kvs[a, 0, k]) for k in range(q + 1)] for q in range(codes)]
+        swap.wait_recv()
+        for q in range(codes):
+            prior = [
+                jnp.where(sec > 0, score(queries[q], kvr[a, 0, k]), -jnp.inf)
+                for k in range(codes)
+            ]
+            every = prior + local[q]
+            top = every[0]
+            for item in every[1:]:
+                top = jnp.maximum(top, item)
+            expo = [jnp.exp(item - top) for item in every]
+            sums = expo[0]
+            for item in expo[1:]:
+                sums = sums + item
+            out = None
+            for k, item in enumerate(expo):
+                value = kvr[a, 1, k] if k < codes else kvs[a, 1, k - codes]
+                term = (item / sums).astype(bf).astype(jnp.float32) * value.astype(jnp.float32)
+                out = term if out is None else out + term
+            mix[a, at_code(q), :] = out.astype(bf)
+
+    def resid_block(a):
+        def block_of(j):
+            return jnp.concatenate(
+                [product(mix[a, at_code(c), :], dout[c, :, features(j)]) for c in range(codes)],
+                axis=0,
+            )
+        return block_of
+
+    def vocab_block(hidden):
+        def block_of(j):
+            there = pl.ds(pl.multiple_of(j * share, share), share)
+            return jnp.concatenate(
+                [product(hidden[at_code(c), :], headw[c, :, there]) for c in range(codes)],
+                axis=0,
+            )
+        return block_of
+
+    both = range(2)
+    blocks = [entry_block(a) for a in both]
+    firsts = [first_sends(1, a, blocks[a], ebuf) for a in both]
+    sums = [second_sends(1, a, blocks[a], ebuf, firsts[a]) for a in both]
+    entry, square_sends, gathers = [], [], []
+    for a in both:
+        entry.append(gathered(a, *sums[a], ebuf))
+        gathers.append(gather_sends(a, entry[a]))
+        square_sends.append(squares_out(0, a, entry[a]))
+    for a in both:
+        gather_forwards(a, *gathers[a])
+    loads["dqkv"].wait()
     loads["dout"].wait()
-    for q in range(codes):
-        prior = [
-            jnp.where(sec > 0, score(queries[q], kvr[0, k]), -jnp.inf) for k in range(codes)
-        ]
-        every = prior + local[q]
-        top = every[0]
-        for item in every[1:]:
-            top = jnp.maximum(top, item)
-        expo = [jnp.exp(item - top) for item in every]
-        sums = expo[0]
-        for item in expo[1:]:
-            sums = sums + item
-        out = None
-        for k, item in enumerate(expo):
-            value = kvr[1, k] if k < codes else kvs[1, k - codes]
-            term = (item / sums).astype(bf).astype(jnp.float32) * value.astype(jnp.float32)
-            out = term if out is None else out + term
-        mix[q * streams:(q + 1) * streams, :] = out.astype(bf)
-
-    def resid_block(j):
-        return jnp.concatenate(
-            [
-                product(mix[c * streams:(c + 1) * streams, :], dout[c, :, features(j)])
-                for c in range(codes)
-            ],
-            axis=0,
-        )
-
-    resid = entry + finished(*summed_over_tp(2, resid_block, dbuf), dbuf)
-    hidden = (resid * hgain_ref[:, features(me)]).astype(bf)
-    sent = squares_out(1, 9, resid)
+    blocks = [resid_block(a) for a in both]
+    firsts = []
+    for a in both:
+        queries, swap = projections(a, gathers[a][1], square_sends[a])
+        attention(a, queries, swap)
+        firsts.append(first_sends(2, a, blocks[a], dbuf))
+    sums = [second_sends(2, a, blocks[a], dbuf, firsts[a]) for a in both]
     loads["headw"].wait()
-    share = headw.shape[2] // n
-
-    def vocab_block(j):
-        there = pl.ds(pl.multiple_of(j * share, share), share)
-        return jnp.concatenate(
-            [product(hidden[c * streams:(c + 1) * streams, :], headw[c, :, there]) for c in range(codes)],
-            axis=0,
-        )
-
-    out = finished(*summed_over_tp(5, vocab_block, lbuf), lbuf)
-    out = out * row_factor(1, sent)[:, :1]
-    logits_ref[...] = out.reshape(codes, streams, share)
+    square_sends, firsts, blocks = [], [], []
+    for a in both:
+        resid = entry[a] + gathered(a, *sums[a], dbuf)
+        hidden = (resid * hgain_ref[:, features(me)]).astype(bf)
+        blocks.append(vocab_block(hidden))
+        firsts.append(first_sends(5, a, blocks[a], lbuf))
+        square_sends.append(squares_out(1, a, resid))
+    sums = [second_sends(5, a, blocks[a], lbuf, firsts[a]) for a in both]
+    for a in both:
+        out = gathered(a, *sums[a], lbuf) * row_factor(1, a, square_sends[a])[:, :1]
+        logits_ref[:, a * s_local:(a + 1) * s_local, :] = out.reshape(codes, s_local, share)
     for copy in pending:
         copy.wait_send()
 
@@ -531,20 +601,20 @@
     scratch = [pltpu.VMEM(a.shape, a.dtype) for a in big] + [
         pltpu.VMEM((4, n // 2, s_local, slim), bf),
         pltpu.VMEM((2, s_local, slim), bf),
-        pltpu.VMEM((total, deep), f32),
-        pltpu.VMEM((4, n // 2, total, part), bf),
-        pltpu.VMEM((n, total, part), bf),
-        pltpu.VMEM((2, codes, streams, lanes), bf),
-        pltpu.VMEM((2, codes, streams, lanes), bf),
-        pltpu.VMEM((total, lanes), bf),
-        pltpu.VMEM((4, n // 2, total, part), bf),
-        pltpu.VMEM((4, n // 2, total, share), bf),
-        pltpu.VMEM((2, n, 8, total), f32),
+        pltpu.VMEM((2, total // 2, deep), f32),
+        pltpu.VMEM((4, 2, n // 2, total // 2, part), bf),
+        pltpu.VMEM((n, 2, total // 2, part), bf),
+        pltpu.VMEM((2, 2, codes, s_local, lanes), bf),
+        pltpu.VMEM((2, 2, codes, s_local, lanes), bf),
+        pltpu.VMEM((2, total // 2, lanes), bf),
+        pltpu.VMEM((4, 2, n // 2, total // 2, part), bf),
+        pltpu.VMEM((4, 2, n // 2, total // 2, share), bf),
+        pltpu.VMEM((2, 2, n, 8, total // 2), f32),
         pltpu.SemaphoreType.DMA((3 * pieces + 8,)),
-        pltpu.SemaphoreType.DMA((12, n)),
-        pltpu.SemaphoreType.DMA((12, n)),
-        pltpu.SemaphoreType.DMA((2,)),
-        pltpu.SemaphoreType.DMA((2,)),
+        pltpu.SemaphoreType.DMA((14, n)),
+        pltpu.SemaphoreType.DMA((14, n)),
+        pltpu.SemaphoreType.DMA((3,)),
+        pltpu.SemaphoreType.DMA((3,)),
     ]
     temporal, logits = pl.pallas_call(
         functools.partial(tick_kernel, n, pieces),
@@ -574,7 +644,7 @@
         and depth_qkv.shape[3] == 128
         and arrays[13].shape[1] % 128 == 0
         and arrays[13].shape[2] % (128 * n) == 0
-        and total % (16 * n) == 0
+        and total % 256 == 0
         and hidden_in.shape[0] % 16 == 0
         and arrays[4].shape[1] <= HEAD_DIM
         and arrays[2].shape[2] <= 8 * HEAD_DIM

time: 80.3 us -> 73.1 us (0.910)
  Pallas kernels: 76.3 us -> 69.1 us
    pallas_call x1, Pallas kernels: 76.3 us -> 69.1 us  [fused(): pl.pallas_call(functools.partial(tick_kernel, n, pieces), out_shape=(jax....]
where the time goes in v1:
time: 73.1 us; the launch traced here: 72.9 us
  Pallas kernels  69.1 us (95%)
  local copies, waits for them, and re-layouts  3.2 us (4%)
    pallas_call x1, Pallas kernels, fused(): pl.pallas_call(functools.partial(tick_kernel, n, pieces), out_shape=(jax....  69.1 us
    unnamed x2, local copies, waits for them, and re-layouts  3.2 us

profile of v1, /device:TPU:0, one launch (start us, length us, event | category | flops | bytes accessed | tf_op | source)
XLA Modules:
  0.0 72.9 jit_solution(3850102067173811993)
XLA Ops:
  0.6 69.1 %shard_map.158 = (bf16[32,512]{1,0:T(8,128)(2,1)}, f32[4,64,256]{2,1,0:T(8,128)}) custom-call(bf16[32,4096]{1,0:T(8,128)(2,1)} %hidden_ref.1, f32[1,4096]{1,0:T(1,128)} %bitcast.7, s32[1,32]{1,0:T(1,128)} %bitcast.11, s32[4,64]{1,0:T(4,128)} %bitcast.10, f32[1,1024]{1,0:T(1,128)} %bitcast.8, f32[1,1024]{1,0:T(1,128)} %bitcast.9, ...), custom_call_target="tpu_custom_call" | custom-call | tf_op jit(solution)/shard_map/pallas_call | solution.py:619
  69.7 1.8 %copy.17 = f32[64,4,256]{2,1,0:T(4,128)} copy(f32[64,4,256]{2,0,1:T(8,128)} %bitcast.6) | data formatting | bytes 524288
  71.5 1.4 %copy.19 = bf16[32,512]{1,0:T(8,128)(2,1)} copy(bf16[32,512]{1,0:T(8,128)(2,1)} %get-tuple-element.10) | data formatting | bytes 65536

commit v2 on v1

--- a/solution.py
+++ b/solution.py
@@ -176,7 +176,7 @@
     qkv_hbm, keys_hbm, values_hbm, outw_hbm, din_hbm, emb_hbm, dqkv_hbm, dout_hbm, headw_hbm,
     temporal_ref, logits_ref,
     qkv, keys, values, outw, din, emb, dqkv, dout, headw,
-    tbuf, rows, ent, ebuf, nrm, kvs, kvr, mix, dbuf, lbuf, squares,
+    tbuf, rows, ent, ebuf, nrm, kvs, kvr, mix, dbuf, lbuf, squares, qs, entry,
     load_sem, send_sem, recv_sem, pair_send, pair_recv,
 ):
     me = lax.axis_index("tp")
@@ -213,12 +213,25 @@
         )
     pl.semaphore_signal(barrier, inc=1, device_id={"section": 1 - sec}, device_id_type=MESH)
 
+    arrivals = {}
+
+    def arrival(phase, d):
+        if phase == 10:
+            phase = 2
+        return arrivals.setdefault((phase, d), len(arrivals))
+
     def to_peer(phase, d, source, target, peer):
         return pltpu.make_async_remote_copy(
             src_ref=source, dst_ref=target,
-            send_sem=send_sem.at[phase, d], recv_sem=recv_sem.at[phase, d],
+            send_sem=send_sem.at[phase], recv_sem=recv_sem.at[arrival(phase, d)],
             device_id={"tp": peer}, device_id_type=MESH,
         )
+
+    def all_came(phase, d, there):
+        to_peer(phase, d, there, there, mate).wait_recv()
+
+    def all_sent(phase, sent):
+        to_peer(phase, 0, sent, sent, mate).wait_send()
 
     def to_partner(phase, source, target):
         return pltpu.make_async_remote_copy(
@@ -227,7 +240,6 @@
             device_id={"section": 1 - sec}, device_id_type=MESH,
         )
 
-    pending = []
     half_n = n // 2
     pair = lax.rem(me, 2)
     spot = me // 2
@@ -248,7 +260,6 @@
                     to_peer(2 * phase, 2 * i + h, buf.at[0, i, at], buf.at[1, i, at], mate)
                 )
                 firsts[-1].start()
-        seconds = []
         for i, d in enumerate(order + [0]):
             target = lax.rem(spot + d, half_n)
             block = block_of(2 * target + pair)
@@ -258,20 +269,14 @@
                 added.append(block[at] + buf[1, i, at].astype(jnp.float32))
                 if d:
                     buf[2, i, at] = added[-1].astype(bf)
-                    seconds.append(
-                        to_peer(
-                            2 * phase + 1, 2 * i + h, buf.at[2, i, at], buf.at[3, i, at],
-                            2 * target + pair,
-                        )
-                    )
-                    seconds[-1].start()
-        pending.extend(firsts + seconds)
-        return jnp.concatenate(added, axis=0), seconds
-
-    def finished(block, seconds, buf):
+                    to_peer(
+                        2 * phase + 1, 0, buf.at[2, i, at], buf.at[3, i, at], 2 * target + pair
+                    ).start()
+        return jnp.concatenate(added, axis=0)
+
+    def finished(phase, block, buf):
+        all_came(2 * phase + 1, 0, buf.at[3, pl.ds(0, half_n - 1)])
         for i in range(half_n - 1):
-            seconds[2 * i].wait_recv()
-            seconds[2 * i + 1].wait_recv()
             block = block + buf[3, i].astype(jnp.float32)
         return block
 
@@ -351,10 +356,9 @@
     def row_block(j):
         return product(mixed, outw[:, pl.ds(pl.multiple_of(j * slim, slim), slim)])
 
-    summed, seconds = summed_over_tp(0, row_block, tbuf)
+    summed = summed_over_tp(0, row_block, tbuf)
 
     vocab = emb.shape[1]
-    chunk_rows = codes * s_local
     loads["emb"].wait()
     ids = lax.broadcasted_iota(jnp.int32, (vocab, streams), 0) + me * vocab
     for c in range(codes):
@@ -363,18 +367,18 @@
             onehot, emb[c], (((0,), (0,)), ((), ())), preferred_element_type=jnp.float32
         )
         for a in range(2):
-            ent[a, c * s_local:(c + 1) * s_local, :] = looked_up[a * s_local:(a + 1) * s_local]
+            ent[lax.rem(a + sec, 2), c * s_local:(c + 1) * s_local, :] = looked_up[
+                a * s_local:(a + 1) * s_local
+            ]
     loads["din"].wait()
 
-    summed = finished(summed, seconds, tbuf)
+    summed = finished(0, summed, tbuf)
     start = pl.multiple_of(me * slim, slim)
     temporal = (hidden_ref[:, pl.ds(start, slim)].astype(jnp.float32) + summed).astype(bf)
     temporal_ref[...] = temporal
-    rows[sec] = temporal
-    swap = to_partner(0, rows.at[sec], rows.at[sec])
-    swap.start()
-    pending.append(swap)
-    swap.wait_recv()
+    rows[0] = temporal
+    row_swap = to_partner(0, rows.at[0], rows.at[1])
+    row_swap.start()
 
     part = din.shape[2] // n
     share = headw.shape[2] // n
@@ -386,42 +390,50 @@
     def features(j):
         return pl.ds(pl.multiple_of(j * part, part), part)
 
-    def first_sends(phase, a, block_of, buf):
-        sent = []
-        for i, d in enumerate(order + [0]):
-            target = lax.rem(spot + d, half_n)
-            buf[0, a, i] = block_of(2 * target + 1 - pair).astype(bf)
-            sent.append(
-                to_peer(2 * phase, 2 * i + a, buf.at[0, a, i], buf.at[1, a, i], mate)
+    class Reduction:
+        def __init__(self, phase, a, block_of, buf):
+            self.phase, self.a, self.block_of, self.buf = phase, a, block_of, buf
+            self.firsts = {}
+
+        def send(self, stage, i, h, at, peer):
+            spot_of = (self.a, i, at)
+            copy = to_peer(
+                2 * self.phase + stage, self.a if stage else 4 * i + 2 * h + self.a,
+                self.buf.at[(2 * stage, *spot_of)], self.buf.at[(2 * stage + 1, *spot_of)], peer,
             )
-            sent[-1].start()
-        pending.extend(sent)
-        return sent
-
-    def second_sends(phase, a, block_of, buf, firsts):
-        sent = []
-        for i, d in enumerate(order + [0]):
-            target = lax.rem(spot + d, half_n)
-            block = block_of(2 * target + pair)
-            firsts[i].wait_recv()
-            block = block + buf[1, a, i].astype(jnp.float32)
-            if d:
-                buf[2, a, i] = block.astype(bf)
-                sent.append(
-                    to_peer(
-                        2 * phase + 1, 2 * i + a, buf.at[2, a, i], buf.at[3, a, i],
-                        2 * target + pair,
-                    )
-                )
-                sent[-1].start()
-        pending.extend(sent)
-        return block, sent
-
-    def gathered(a, block, sent, buf):
-        for i in range(half_n - 1):
-            sent[i].wait_recv()
-            block = block + buf[3, a, i].astype(jnp.float32)
-        return block
+            copy.start()
+            return copy
+
+        def start(self):
+            for i, d in enumerate(order + [0]):
+                target = lax.rem(spot + d, half_n)
+                self.buf[0, self.a, i] = self.block_of(2 * target + 1 - pair).astype(bf)
+                for h, at in halves(self.buf.shape[3]):
+                    self.firsts[i, h] = self.send(0, i, h, at, mate)
+
+        def forward(self):
+            for i, d in enumerate(order + [0]):
+                target = lax.rem(spot + d, half_n)
+                block = self.block_of(2 * target + pair)
+                added = []
+                for h, at in halves(self.buf.shape[3]):
+                    self.firsts[i, h].wait_recv()
+                    added.append(block[at] + self.buf[1, self.a, i, at].astype(jnp.float32))
+                    if d:
+                        self.buf[2, self.a, i, at] = added[-1].astype(bf)
+                        self.send(1, i, h, at, 2 * target + pair)
+            self.own = jnp.concatenate(added, axis=0)
+
+        def result(self):
+            block = self.own
+            all_came(2 * self.phase + 1, self.a, self.buf.at[3, self.a, pl.ds(0, half_n - 1)])
+            for i in range(half_n - 1):
+                block = block + self.buf[3, self.a, i].astype(jnp.float32)
+            return block
+
+        def drain(self):
+            all_sent(2 * self.phase, self.buf.at[0, self.a])
+            all_sent(2 * self.phase + 1, self.buf.at[2, self.a, pl.ds(0, half_n - 1)])
 
     def entry_block(a):
         def block_of(j):
@@ -437,21 +449,14 @@
 
     def squares_out(which, a, block):
         squares[which, a, me] = row_squares(block)
-        sent = []
         for d in range(1, n):
-            sent.append(
-                to_peer(
-                    8 + which + 4 * a, d, squares.at[which, a, me], squares.at[which, a, me],
-                    lax.rem(me + d, n),
-                )
-            )
-            sent[-1].start()
-        pending.extend(sent)
-        return sent
-
-    def row_factor(which, a, sent):
-        for copy in sent:
-            copy.wait_recv()
+            to_peer(
+                8 + which + 4 * a, 0, squares.at[which, a, me], squares.at[which, a, me],
+                lax.rem(me + d, n),
+            ).start()
+
+    def row_factor(which, a):
+        all_came(8 + which + 4 * a, 0, squares.at[which, a, pl.ds(0, n - 1)])
         mean = jnp.sum(squares[which, a], axis=0) / (n * part)
         column = lax.dot_general(
             mean, jnp.full((8, 128), 0.125, jnp.float32), (((0,), (0,)), ((), ())),
@@ -459,61 +464,71 @@
         )
         return lax.rsqrt(column + EPSILON)
 
-    def gather_sends(a, block):
-        nrm[me, a] = (block * dgain_ref[:, features(me)]).astype(bf)
-        copies = []
-        for i, d in enumerate(order):
-            peer = 2 * lax.rem(spot + d, half_n) + pair
-            copies.append(to_peer(6, 2 * i + a, nrm.at[me, a], nrm.at[me, a], peer))
-            copies[-1].start()
-        swaps = [to_peer(6, n - 2 + a, nrm.at[me, a], nrm.at[me, a], mate)]
-        swaps[0].start()
-        return copies, swaps
-
-    def gather_forwards(a, copies, swaps):
-        for i, d in enumerate(order):
-            came = 2 * lax.rem(spot - d + half_n, half_n) + pair
-            copies[i].wait_recv()
-            swaps.append(to_peer(7, 2 * i + a, nrm.at[came, a], nrm.at[came, a], mate))
-            swaps[-1].start()
-        pending.extend(copies + swaps)
-
-    def projections(a, swaps, sent):
-        r = row_factor(0, a, sent)
-        for copy in swaps:
-            copy.wait_recv()
-        queries = []
+    class Gather:
+        def __init__(self, a):
+            self.a = a
+            self.copies = []
+
+        def send(self, phase, i, place, peer):
+            there = nrm.at[place, self.a]
+            copy = to_peer(phase, 2 * i + self.a, there, there, peer)
+            copy.start()
+            return copy
+
+        def start(self, block):
+            nrm[me, self.a] = (block * dgain_ref[:, features(me)]).astype(bf)
+            for i, d in enumerate(order):
+                peer = 2 * lax.rem(spot + d, half_n) + pair
+                self.copies.append(self.send(6, i, me, peer))
+            self.send(7, 0, me, mate)
+
+        def forward(self):
+            for i, d in enumerate(order):
+                came = 2 * lax.rem(spot - d + half_n, half_n) + pair
+                self.copies[i].wait_recv()
+                self.send(7, 0, came, mate)
+
+    def projections(a, r):
+        all_came(7, a, nrm.at[pl.ds(0, half_n), a])
+        chunk = lax.rem(a + sec, 2)
         for c in range(codes):
             x = jnp.concatenate([nrm[j, a, at_code(c), :] for j in range(n)], axis=1)
             f = r[at_code(c)]
-            queries.append((product(x, dqkv[c, 0]) * f).astype(bf).astype(jnp.float32))
-            kvs[a, 0, c] = (product(x, dqkv[c, 1]) * f).astype(bf)
-            kvs[a, 1, c] = (product(x, dqkv[c, 2]) * f).astype(bf)
-        swap = to_partner(1 + a, kvs.at[a], kvr.at[a])
-        swap.start()
-        pending.append(swap)
-        return queries, swap
+            qs[chunk, c] = (product(x, dqkv[c, 0]) * f).astype(bf)
+            kvs[chunk, 0, c] = (product(x, dqkv[c, 1]) * f).astype(bf)
+            kvs[chunk, 1, c] = (product(x, dqkv[c, 2]) * f).astype(bf)
+        to_partner(1 + chunk, kvs.at[chunk], kvr.at[chunk]).start()
 
     row_head = lax.rem(lax.broadcasted_iota(jnp.int32, (2 * lanes, lanes), 0), lanes) // DEPTH_HDIM
     col_head = lax.broadcasted_iota(jnp.int32, (2 * lanes, lanes), 1) // DEPTH_HDIM
     ones = jnp.where(row_head == col_head, 1.0, 0.0).astype(bf)
     scale = 1.0 / math.sqrt(DEPTH_HDIM)
 
-    def score(query, key):
-        both = query * key.astype(jnp.float32)
+    def scores(queries, keys):
+        both = jnp.concatenate(
+            [query * key.astype(jnp.float32) for query, key in zip(queries, keys)], axis=0
+        )
         high = both.astype(bf)
         low = (both - high.astype(jnp.float32)).astype(bf)
-        return product(jnp.concatenate([high, low], axis=1), ones) * scale
-
-    def attention(a, queries, swap):
-        local = [[score(queries[q], kvs[a, 0, k]) for k in range(q + 1)] for q in range(codes)]
+        out = product(jnp.concatenate([high, low], axis=1), ones) * scale
+        return [out[i * s_local:(i + 1) * s_local] for i in range(len(queries))]
+
+    partner_swaps = [row_swap]
+
+    def attention(a):
+        queries = [qs[a, c].astype(jnp.float32) for c in range(codes)]
+        pairs = [(q, k) for q in range(codes) for k in range(q + 1)]
+        local = scores([queries[q] for q, _ in pairs], [kvs[a, 0, k] for _, k in pairs])
+        local = dict(zip(pairs, local))
+        swap = to_partner(1 + a, kvs.at[a], kvr.at[a])
         swap.wait_recv()
+        partner_swaps.append(swap)
+        pairs = [(q, k) for q in range(codes) for k in range(codes)]
+        prior = scores([queries[q] for q, _ in pairs], [kvr[a, 0, k] for _, k in pairs])
+        prior = dict(zip(pairs, prior))
         for q in range(codes):
-            prior = [
-                jnp.where(sec > 0, score(queries[q], kvr[a, 0, k]), -jnp.inf)
-                for k in range(codes)
-            ]
-            every = prior + local[q]
+            every = [jnp.where(sec > 0, prior[q, k], -jnp.inf) for k in range(codes)]
+            every += [local[q, k] for k in range(q + 1)]
             top = every[0]
             for item in every[1:]:
                 top = jnp.maximum(top, item)
@@ -545,40 +560,67 @@
             )
         return block_of
 
-    both = range(2)
-    blocks = [entry_block(a) for a in both]
-    firsts = [first_sends(1, a, blocks[a], ebuf) for a in both]
-    sums = [second_sends(1, a, blocks[a], ebuf, firsts[a]) for a in both]
-    entry, square_sends, gathers = [], [], []
-    for a in both:
-        entry.append(gathered(a, *sums[a], ebuf))
-        gathers.append(gather_sends(a, entry[a]))
-        square_sends.append(squares_out(0, a, entry[a]))
-    for a in both:
-        gather_forwards(a, *gathers[a])
+    entries = [Reduction(1, a, entry_block(a), ebuf) for a in range(2)]
+    entries[0].start()
+    row_swap.wait_recv()
+    entries[1].start()
+    entries[0].forward()
+    entries[1].forward()
+    gathers = [Gather(a) for a in range(2)]
+    for a in range(2):
+        block = entries[a].result()
+        squares_out(0, a, block)
+        gathers[a].start(block)
+        entry[lax.rem(a + sec, 2)] = block
+    gathers[0].forward()
+    gathers[1].forward()
     loads["dqkv"].wait()
     loads["dout"].wait()
-    blocks = [resid_block(a) for a in both]
-    firsts = []
-    for a in both:
-        queries, swap = projections(a, gathers[a][1], square_sends[a])
-        attention(a, queries, swap)
-        firsts.append(first_sends(2, a, blocks[a], dbuf))
-    sums = [second_sends(2, a, blocks[a], dbuf, firsts[a]) for a in both]
+    for a in range(2):
+        factor = row_factor(0, a)
+        projections(a, factor)
+    resids = [Reduction(2, a, resid_block(a), dbuf) for a in range(2)]
+    for a in range(2):
+        attention(a)
+        resids[a].start()
+    resids[0].forward()
+    resids[1].forward()
     loads["headw"].wait()
-    square_sends, firsts, blocks = [], [], []
-    for a in both:
-        resid = entry[a] + gathered(a, *sums[a], dbuf)
+    heads_of = []
+    for a in range(2):
+        resid = entry[a] + resids[a].result()
+        squares_out(1, a, resid)
         hidden = (resid * hgain_ref[:, features(me)]).astype(bf)
-        blocks.append(vocab_block(hidden))
-        firsts.append(first_sends(5, a, blocks[a], lbuf))
-        square_sends.append(squares_out(1, a, resid))
-    sums = [second_sends(5, a, blocks[a], lbuf, firsts[a]) for a in both]
-    for a in both:
-        out = gathered(a, *sums[a], lbuf) * row_factor(1, a, square_sends[a])[:, :1]
+        heads_of.append(Reduction(5, a, vocab_block(hidden), lbuf))
+        heads_of[a].start()
+    heads_of[0].forward()
+    factors = [row_factor(1, a) for a in range(2)]
+    heads_of[1].forward()
+    for a in range(2):
+        out = heads_of[a].result() * factors[a][:, :1]
         logits_ref[:, a * s_local:(a + 1) * s_local, :] = out.reshape(codes, s_local, share)
-    for copy in pending:
+    all_sent(0, tbuf.at[0])
+    all_sent(1, tbuf.at[2, pl.ds(0, half_n - 1)])
+    for item in entries + resids + heads_of:
+        item.drain()
+    all_sent(6, nrm.at[pl.ds(0, half_n - 1)])
+    all_sent(7, nrm.at[pl.ds(0, half_n)])
+    for which in range(2):
+        for a in range(2):
+            all_sent(8 + which + 4 * a, squares.at[which, a, pl.ds(0, n - 1)])
+    for copy in partner_swaps:
         copy.wait_send()
+    assert len(arrivals) <= recv_sem.shape[0]
+
+
+def deliver_kernel(temporal_ref, logits_ref, temporal_hbm, logits_hbm, turned, sems):
+    first = pltpu.make_async_copy(temporal_ref, temporal_hbm, sems.at[0])
+    first.start()
+    turned[...] = jnp.swapaxes(logits_ref[...], 0, 1)
+    second = pltpu.make_async_copy(turned, logits_hbm, sems.at[1])
+    second.start()
+    first.wait()
+    second.wait()
 
 
 def fused(
@@ -610,17 +652,19 @@
         pltpu.VMEM((4, 2, n // 2, total // 2, part), bf),
         pltpu.VMEM((4, 2, n // 2, total // 2, share), bf),
         pltpu.VMEM((2, 2, n, 8, total // 2), f32),
+        pltpu.VMEM((2, codes, s_local, lanes), bf),
+        pltpu.VMEM((2, total // 2, part), f32),
         pltpu.SemaphoreType.DMA((3 * pieces + 8,)),
-        pltpu.SemaphoreType.DMA((14, n)),
-        pltpu.SemaphoreType.DMA((14, n)),
+        pltpu.SemaphoreType.DMA((14,)),
+        pltpu.SemaphoreType.DMA((7 * n + 4,)),
         pltpu.SemaphoreType.DMA((3,)),
         pltpu.SemaphoreType.DMA((3,)),
     ]
     temporal, logits = pl.pallas_call(
         functools.partial(tick_kernel, n, pieces),
         out_shape=(
-            jax.ShapeDtypeStruct((s_local, slim), bf),
-            jax.ShapeDtypeStruct((codes, streams, share), f32),
+            pltpu.VMEM((s_local, slim), bf),
+            pltpu.VMEM((codes, streams, share), f32),
         ),
         in_specs=[vmem] * 6 + [pl.BlockSpec(memory_space=pl.ANY)] * 9,
         out_specs=(vmem, vmem),
@@ -632,7 +676,20 @@
         hidden_in, temporal_gain[None, :], lengths[None, :], tokens.T, depth_gain[None, :], head_gain[None, :],
         *big,
     )
-    return temporal, jnp.swapaxes(logits, 0, 1)
+    return pl.pallas_call(
+        deliver_kernel,
+        out_shape=(
+            jax.ShapeDtypeStruct((s_local, slim), bf),
+            jax.ShapeDtypeStruct((streams, codes, share), f32),
+        ),
+        in_specs=[vmem] * 2,
+        out_specs=(pl.BlockSpec(memory_space=pl.ANY),) * 2,
+        scratch_shapes=[
+            pltpu.VMEM((streams, codes, share), f32),
+            pltpu.SemaphoreType.DMA((2,)),
+        ],
+        compiler_params=pltpu.CompilerParams(vmem_limit_bytes=2 * 1024 * 1024),
+    )(temporal, logits)
 
 
 def fits(n, arrays):
@@ -640,10 +697,10 @@
     total = depth_in.shape[0] * 2 * hidden_in.shape[0]
     return (
         lax.axis_size("section") == 2
-        and n % 2 == 0
         and depth_qkv.shape[3] == 128
         and arrays[13].shape[1] % 128 == 0
         and arrays[13].shape[2] % (128 * n) == 0
+        and n % 2 == 0
         and total % 256 == 0
         and hidden_in.shape[0] % 16 == 0
         and arrays[4].shape[1] <= HEAD_DIM

time: 73.1 us -> 67.4 us (0.922)
  local copies, waits for them, and re-layouts: 3.2 us -> 0 us
  Pallas kernels: 69.1 us -> 66.6 us
    unnamed x2 -> x0, local copies, waits for them, and re-layouts: 3.2 us -> none
    pallas_call x1 -> x2, Pallas kernels: 69.1 us -> 66.6 us  [the longest x1 65.8 us: fused(): pl.pallas_call(functools.partial(tick_kernel, n, pieces), out_shape=(pltp...]
where the time goes in v2:
time: 67.4 us; the launch traced here: 67.2 us
  Pallas kernels  66.6 us (99%)
    pallas_call x1, Pallas kernels, fused(): pl.pallas_call(functools.partial(tick_kernel, n, pieces), out_shape=(pltp...  65.8 us

profile of v2, /device:TPU:0, one launch (start us, length us, event | category | flops | bytes accessed | tf_op | source)
XLA Modules:
  0.0 67.2 jit_solution(10560146221260655343)
XLA Ops:
  0.6 65.8 %shard_map.158 = (bf16[32,512]{1,0:T(8,128)(2,1)S(1)}, f32[4,64,256]{2,1,0:T(8,128)S(1)}) custom-call(bf16[32,4096]{1,0:T(8,128)(2,1)} %hidden_ref.1, f32[1,4096]{1,0:T(1,128)} %bitcast.5, s32[1,32]{1,0:T(1,128)} %bitcast.9, s32[4,64]{1,0:T(4,128)} %bitcast.8, f32[1,1024]{1,0:T(1,128)} %bitcast.6, f32[1,1024]{1,0:T(1,128)} %bitcast.7, ...), custom_call_target="tpu_custom_call" | custom-call | tf_op jit(solution)/shard_map/pallas_call | solution.py:663
  66.4 0.8 %shard_map.159 = (bf16[32,512]{1,0:T(8,128)(2,1)}, f32[64,4,256]{2,1,0:T(4,128)}) custom-call(bf16[32,512]{1,0:T(8,128)(2,1)S(1)} %get-tuple-element.4.temporal_ref, f32[4,64,256]{2,1,0:T(8,128)S(1)} %get-tuple-element.5.logits_ref), custom_call_target="tpu_custom_call" | custom-call | tf_op jit(solution)/shard_map/pallas_call | solution.py:679

commit v3 on v2

--- a/solution.py
+++ b/solution.py
@@ -172,9 +172,10 @@
 
 def tick_kernel(
     n, pieces,
-    hidden_ref, gain_ref, lens_ref, tokens_ref, dgain_ref, hgain_ref,
+    hidden_hbm, gain_hbm, lens_hbm, tokens_hbm, dgain_hbm, hgain_hbm,
     qkv_hbm, keys_hbm, values_hbm, outw_hbm, din_hbm, emb_hbm, dqkv_hbm, dout_hbm, headw_hbm,
     temporal_ref, logits_ref,
+    hidden_ref, gain_ref, lens_ref, tokens_ref, dgain_ref, hgain_ref,
     qkv, keys, values, outw, din, emb, dqkv, dout, headw,
     tbuf, rows, ent, ebuf, nrm, kvs, kvr, mix, dbuf, lbuf, squares, qs, entry,
     load_sem, send_sem, recv_sem, pair_send, pair_recv,
@@ -199,13 +200,23 @@
         loads[name].start()
         slot += 1
 
-    for t in range(3):
+    def load_weights(t):
         for k in range(pieces):
             part = pl.ds(k * span, span)
             load(("qkv", t, k), qkv_hbm.at[t, part, :], qkv.at[t, part, :])
+
+    load("hidden", hidden_hbm, hidden_ref)
+    load("gain", gain_hbm, gain_ref)
+    load("lens", lens_hbm, lens_ref)
+    load_weights(0)
     load("keys", keys_hbm, keys)
+    load_weights(1)
     load("values", values_hbm, values)
+    load_weights(2)
     load("outw", outw_hbm, outw)
+    load("tokens", tokens_hbm, tokens_ref)
+    load("dgain", dgain_hbm, dgain_ref)
+    load("hgain", hgain_hbm, hgain_ref)
     barrier = pltpu.get_barrier_semaphore()
     for d in range(1, n):
         pl.semaphore_signal(
@@ -280,6 +291,8 @@
             block = block + buf[3, i].astype(jnp.float32)
         return block
 
+    for name in ("hidden", "gain", "lens"):
+        loads[name].wait()
     normed = normalised(hidden_ref[...].astype(jnp.float32), gain_ref[...]).astype(bf)
     half = HEAD_DIM // 2
     lane = lax.broadcasted_iota(jnp.int32, (s_local, HEAD_DIM), 1)
@@ -295,59 +308,70 @@
     cosine = jnp.cos(angles)
     sine = jnp.sin(angles)
     sine = jnp.where(lane < half, -sine, sine)
-    proj = []
-    for t in range(3):
+
+    def projected(t):
         acc = None
         for k in range(pieces):
             loads["qkv", t, k].wait()
             term = product(normed[:, k * span:(k + 1) * span], qkv[t, k * span:(k + 1) * span, :])
             acc = term if acc is None else acc + term
-        if t == 1:
-            load("emb", emb_hbm, emb)
-            load("din", din_hbm, din)
-            load("dqkv", dqkv_hbm, dqkv)
-            load("dout", dout_hbm, dout)
-            load("headw", headw_hbm, headw)
         if t < 2:
             turned = []
             for h in range(heads):
                 one = acc[:, h * HEAD_DIM:(h + 1) * HEAD_DIM]
                 turned.append(one * cosine + pltpu.roll(one, half, 1) * sine)
             acc = jnp.concatenate(turned, axis=1)
-        proj.append(acc.astype(bf).astype(jnp.float32))
+        return acc.astype(bf).astype(jnp.float32)
 
     factor = 1.0 / math.sqrt(HEAD_DIM)
-    loads["keys"].wait()
-    loads["values"].wait()
     group = 8
     padded = 8
     owner = lax.broadcasted_iota(jnp.int32, (group, padded, cols), 2) // HEAD_DIM
     mine = owner == lax.broadcasted_iota(jnp.int32, (group, padded, cols), 1)
     place = lax.broadcasted_iota(jnp.int32, (group, padded, cache_len), 2).astype(jnp.float32)
-    mixed = []
-    for g in range(s_local // group):
-        at = slice(g * group, (g + 1) * group)
-        q_g = jnp.where(mine, proj[0][at][:, None, :], 0.0)
-        scores = lax.dot_general(
-            q_g.astype(bf), keys[at], (((2,), (2,)), ((0,), (0,))),
-            preferred_element_type=jnp.float32,
+    groups = [slice(g * group, (g + 1) * group) for g in range(s_local // group)]
+
+    queries = projected(0)
+    loads["keys"].wait()
+    cached = []
+    for at in groups:
+        q_g = jnp.where(mine, queries[at][:, None, :], 0.0)
+        cached.append(
+            lax.dot_general(
+                q_g.astype(bf), keys[at], (((2,), (2,)), ((0,), (0,))),
+                preferred_element_type=jnp.float32,
+            ) * factor
+        )
+    new_keys = projected(1)
+    load("emb", emb_hbm, emb)
+    load("din", din_hbm, din)
+    load("dqkv", dqkv_hbm, dqkv)
+    load("dout", dout_hbm, dout)
+    load("headw", headw_hbm, headw)
+    weights, own_weights = [], []
+    for at, scores in zip(groups, cached):
+        own_score = jnp.sum(
+            jnp.where(mine, (queries[at] * new_keys[at])[:, None, :], 0.0), axis=-1, keepdims=True
         ) * factor
-        own_score = jnp.sum(q_g * proj[1][at][:, None, :], axis=-1, keepdims=True) * factor
         live = place < lens[at, :cache_len][:, None, :]
         scores = jnp.where(live, scores, -jnp.inf)
         highest = jnp.maximum(jnp.max(scores, axis=-1, keepdims=True), own_score)
         expo = jnp.exp(scores - highest)
         own_expo = jnp.exp(own_score - highest)
         totals = jnp.sum(expo, axis=-1, keepdims=True) + own_expo
-        weights = (expo / totals).astype(bf)
+        weights.append((expo / totals).astype(bf))
         own_weight = (own_expo / totals).astype(bf).astype(jnp.float32)
+        own_weights.append(jnp.sum(jnp.where(mine, own_weight, 0.0), axis=1))
+    loads["values"].wait()
+    mixed = []
+    for at, weight in zip(groups, weights):
         out = lax.dot_general(
-            weights, values[at], (((2,), (1,)), ((0,), (0,))),
-            preferred_element_type=jnp.float32,
-        )
-        out = jnp.where(mine, out + own_weight * proj[2][at][:, None, :], 0.0)
-        mixed.append(jnp.sum(out, axis=1))
-    mixed = jnp.concatenate(mixed, axis=0).astype(bf)
+            weight, values[at], (((2,), (1,)), ((0,), (0,))), preferred_element_type=jnp.float32
+        )
+        mixed.append(jnp.sum(jnp.where(mine, out, 0.0), axis=1))
+    mixed = jnp.concatenate(mixed, axis=0)
+    own_weights = jnp.concatenate(own_weights, axis=0)
+    mixed = (mixed + own_weights * projected(2)).astype(bf)
 
     loads["outw"].wait()
     slim = width // n
@@ -359,7 +383,8 @@
     summed = summed_over_tp(0, row_block, tbuf)
 
     vocab = emb.shape[1]
-    loads["emb"].wait()
+    for name in ("emb", "tokens", "dgain", "hgain"):
+        loads[name].wait()
     ids = lax.broadcasted_iota(jnp.int32, (vocab, streams), 0) + me * vocab
     for c in range(codes):
         onehot = jnp.where(tokens_ref[c:c + 1, :] == ids, 1.0, 0.0).astype(bf)
@@ -639,8 +664,10 @@
     pieces = 4
     big = [temporal_qkv, cache_keys, cache_values, temporal_out_weight, depth_in, depth_embed,
            depth_qkv, depth_out_weight, head_weight]
+    small = [hidden_in, temporal_gain[None, :], lengths[None, :], tokens.T, depth_gain[None, :],
+             head_gain[None, :]]
     vmem = pl.BlockSpec(memory_space=pltpu.VMEM)
-    scratch = [pltpu.VMEM(a.shape, a.dtype) for a in big] + [
+    scratch = [pltpu.VMEM(a.shape, a.dtype) for a in small + big] + [
         pltpu.VMEM((4, n // 2, s_local, slim), bf),
         pltpu.VMEM((2, s_local, slim), bf),
         pltpu.VMEM((2, total // 2, deep), f32),
@@ -654,7 +681,7 @@
         pltpu.VMEM((2, 2, n, 8, total // 2), f32),
         pltpu.VMEM((2, codes, s_local, lanes), bf),
         pltpu.VMEM((2, total // 2, part), f32),
-        pltpu.SemaphoreType.DMA((3 * pieces + 8,)),
+        pltpu.SemaphoreType.DMA((3 * pieces + 14,)),
         pltpu.SemaphoreType.DMA((14,)),
         pltpu.SemaphoreType.DMA((7 * n + 4,)),
         pltpu.SemaphoreType.DMA((3,)),
@@ -666,15 +693,14 @@
             pltpu.VMEM((s_local, slim), bf),
             pltpu.VMEM((codes, streams, share), f32),
         ),
-        in_specs=[vmem] * 6 + [pl.BlockSpec(memory_space=pl.ANY)] * 9,
+        in_specs=[pl.BlockSpec(memory_space=pl.ANY)] * 15,
         out_specs=(vmem, vmem),
         scratch_shapes=scratch,
         compiler_params=pltpu.CompilerParams(
             collective_id=0, has_side_effects=True, vmem_limit_bytes=60 * 1024 * 1024
         ),
     )(
-        hidden_in, temporal_gain[None, :], lengths[None, :], tokens.T, depth_gain[None, :], head_gain[None, :],
-        *big,
+        *small, *big,
     )
     return pl.pallas_call(
         deliver_kernel,

time: 67.4 us -> 65.6 us (0.973)
  Pallas kernels: 66.6 us -> 64.8 us
    pallas_call x1, Pallas kernels: 65.8 us -> 64 us  [fused(): pl.pallas_call(functools.partial(tick_kernel, n, pieces), out_shape=(pltp...]
where the time goes in v3:
time: 65.6 us; the launch traced here: 65.4 us
  Pallas kernels  64.8 us (99%)
    pallas_call x1, Pallas kernels, fused(): pl.pallas_call(functools.partial(tick_kernel, n, pieces), out_shape=(pltp...  64 us

profile of v3, /device:TPU:0, one launch (start us, length us, event | category | flops | bytes accessed | tf_op | source)
XLA Modules:
  0.0 65.4 jit_solution(2535793301739066576)
XLA Ops:
  0.6 64.0 %shard_map.158 = (bf16[32,512]{1,0:T(8,128)(2,1)S(1)}, f32[4,64,256]{2,1,0:T(8,128)S(1)}) custom-call(bf16[32,4096]{1,0:T(8,128)(2,1)} %hidden_hbm.1, f32[1,4096]{1,0:T(1,128)} %bitcast.5, s32[1,32]{1,0:T(1,128)} %bitcast.9, s32[4,64]{1,0:T(4,128)} %bitcast.8, f32[1,1024]{1,0:T(1,128)} %bitcast.6, f32[1,1024]{1,0:T(1,128)} %bitcast.7, ...), custom_call_target="tpu_custom_call" | custom-call | tf_op jit(solution)/shard_map/pallas_call | solution.py:690
  64.7 0.8 %shard_map.159 = (bf16[32,512]{1,0:T(8,128)(2,1)}, f32[64,4,256]{2,1,0:T(4,128)}) custom-call(bf16[32,512]{1,0:T(8,128)(2,1)S(1)} %get-tuple-element.4.temporal_ref, f32[4,64,256]{2,1,0:T(8,128)S(1)} %get-tuple-element.5.logits_ref), custom_call_target="tpu_custom_call" | custom-call | tf_op jit(solution)/shard_map/pallas_call | solution.py:705

commit v4 on v3

--- a/solution.py
+++ b/solution.py
@@ -415,6 +415,8 @@
     def features(j):
         return pl.ds(pl.multiple_of(j * part, part), part)
 
+    turns = order + [0]
+
     class Reduction:
         def __init__(self, phase, a, block_of, buf):
             self.phase, self.a, self.block_of, self.buf = phase, a, block_of, buf
@@ -429,25 +431,31 @@
             copy.start()
             return copy
 
+        def start_one(self, i):
+            target = lax.rem(spot + turns[i], half_n)
+            self.buf[0, self.a, i] = self.block_of(2 * target + 1 - pair).astype(bf)
+            for h, at in halves(self.buf.shape[3]):
+                self.firsts[i, h] = self.send(0, i, h, at, mate)
+
+        def forward_one(self, i):
+            target = lax.rem(spot + turns[i], half_n)
+            block = self.block_of(2 * target + pair)
+            added = []
+            for h, at in halves(self.buf.shape[3]):
+                self.firsts[i, h].wait_recv()
+                added.append(block[at] + self.buf[1, self.a, i, at].astype(jnp.float32))
+                if turns[i]:
+                    self.buf[2, self.a, i, at] = added[-1].astype(bf)
+                    self.send(1, i, h, at, 2 * target + pair)
+            self.own = jnp.concatenate(added, axis=0)
+
         def start(self):
-            for i, d in enumerate(order + [0]):
-                target = lax.rem(spot + d, half_n)
-                self.buf[0, self.a, i] = self.block_of(2 * target + 1 - pair).astype(bf)
-                for h, at in halves(self.buf.shape[3]):
-                    self.firsts[i, h] = self.send(0, i, h, at, mate)
+            for i in range(half_n):
+                self.start_one(i)
 
         def forward(self):
-            for i, d in enumerate(order + [0]):
-                target = lax.rem(spot + d, half_n)
-                block = self.block_of(2 * target + pair)
-                added = []
-                for h, at in halves(self.buf.shape[3]):
-                    self.firsts[i, h].wait_recv()
-                    added.append(block[at] + self.buf[1, self.a, i, at].astype(jnp.float32))
-                    if d:
-                        self.buf[2, self.a, i, at] = added[-1].astype(bf)
-                        self.send(1, i, h, at, 2 * target + pair)
-            self.own = jnp.concatenate(added, axis=0)
+            for i in range(half_n):
+                self.forward_one(i)
 
         def result(self):
             block = self.own
@@ -507,11 +515,14 @@
                 self.copies.append(self.send(6, i, me, peer))
             self.send(7, 0, me, mate)
 
+        def forward_one(self, i):
+            came = 2 * lax.rem(spot - order[i] + half_n, half_n) + pair
+            self.copies[i].wait_recv()
+            self.send(7, 0, came, mate)
+
         def forward(self):
-            for i, d in enumerate(order):
-                came = 2 * lax.rem(spot - d + half_n, half_n) + pair
-                self.copies[i].wait_recv()
-                self.send(7, 0, came, mate)
+            for i in range(half_n - 1):
+                self.forward_one(i)
 
     def projections(a, r):
         all_came(7, a, nrm.at[pl.ds(0, half_n), a])
@@ -588,21 +599,28 @@
     entries = [Reduction(1, a, entry_block(a), ebuf) for a in range(2)]
     entries[0].start()
     row_swap.wait_recv()
-    entries[1].start()
-    entries[0].forward()
+    for i in range(half_n):
+        entries[1].start_one(i)
+        if i:
+            entries[0].forward_one(i - 1)
+    entries[0].forward_one(half_n - 1)
     entries[1].forward()
     gathers = [Gather(a) for a in range(2)]
     for a in range(2):
         block = entries[a].result()
+        gathers[a].start(block)
         squares_out(0, a, block)
-        gathers[a].start(block)
         entry[lax.rem(a + sec, 2)] = block
     gathers[0].forward()
-    gathers[1].forward()
+    for i in range(half_n - 1):
+        if i == half_n - 2:
+            factor = row_factor(0, 0)
+        gathers[1].forward_one(i)
     loads["dqkv"].wait()
     loads["dout"].wait()
     for a in range(2):
-        factor = row_factor(0, a)
+        if a:
+            factor = row_factor(0, a)
         projections(a, factor)
     resids = [Reduction(2, a, resid_block(a), dbuf) for a in range(2)]
     for a in range(2):
@@ -614,13 +632,16 @@
     heads_of = []
     for a in range(2):
         resid = entry[a] + resids[a].result()
-        squares_out(1, a, resid)
+        if a:
+            squares_out(1, a, resid)
         hidden = (resid * hgain_ref[:, features(me)]).astype(bf)
         heads_of.append(Reduction(5, a, vocab_block(hidden), lbuf))
         heads_of[a].start()
+        if not a:
+            squares_out(1, a, resid)
     heads_of[0].forward()
+    heads_of[1].forward()
     factors = [row_factor(1, a) for a in range(2)]
-    heads_of[1].forward()
     for a in range(2):
         out = heads_of[a].result() * factors[a][:, :1]
         logits_ref[:, a * s_local:(a + 1) * s_local, :] = out.reshape(codes, s_local, share)

time: 65.6 us -> 64.8 us (0.988)
  Pallas kernels: 64.8 us -> 64 us
    pallas_call x1, Pallas kernels: 64 us -> 63.3 us  [fused(): pl.pallas_call(functools.partial(tick_kernel, n, pieces), out_shape=(pltp...]
where the time goes in v4:
time: 64.8 us; the launch traced here: 64.7 us
  Pallas kernels  64 us (99%)
    pallas_call x1, Pallas kernels, fused(): pl.pallas_call(functools.partial(tick_kernel, n, pieces), out_shape=(pltp...  63.3 us

profile of v4, /device:TPU:0, one launch (start us, length us, event | category | flops | bytes accessed | tf_op | source)
XLA Modules:
  0.0 64.7 jit_solution(3649587472752440471)
XLA Ops:
  0.6 63.3 %shard_map.158 = (bf16[32,512]{1,0:T(8,128)(2,1)S(1)}, f32[4,64,256]{2,1,0:T(8,128)S(1)}) custom-call(bf16[32,4096]{1,0:T(8,128)(2,1)} %hidden_hbm.1, f32[1,4096]{1,0:T(1,128)} %bitcast.5, s32[1,32]{1,0:T(1,128)} %bitcast.9, s32[4,64]{1,0:T(4,128)} %bitcast.8, f32[1,1024]{1,0:T(1,128)} %bitcast.6, f32[1,1024]{1,0:T(1,128)} %bitcast.7, ...), custom_call_target="tpu_custom_call" | custom-call | tf_op jit(solution)/shard_map/pallas_call | solution.py:711
  63.9 0.8 %shard_map.159 = (bf16[32,512]{1,0:T(8,128)(2,1)}, f32[64,4,256]{2,1,0:T(4,128)}) custom-call(bf16[32,512]{1,0:T(8,128)(2,1)S(1)} %get-tuple-element.4.temporal_ref, f32[4,64,256]{2,1,0:T(8,128)S(1)} %get-tuple-element.5.logits_ref), custom_call_target="tpu_custom_call" | custom-call | tf_op jit(solution)/shard_map/pallas_call | solution.py:726

commit v5 on v4

--- a/solution.py
+++ b/solution.py
@@ -200,6 +200,16 @@
         loads[name].start()
         slot += 1
 
+    half_n = n // 2
+    pair = lax.rem(me, 2)
+    spot = me // 2
+    mate = 2 * spot + 1 - pair
+    order = sorted(range(1, half_n), key=lambda d: abs(d - half_n // 2))
+    slim = width // n
+
+    def row_columns(j):
+        return pl.ds(pl.multiple_of(j * slim, slim), slim)
+
     def load_weights(t):
         for k in range(pieces):
             part = pl.ds(k * span, span)
@@ -213,7 +223,10 @@
     load_weights(1)
     load("values", values_hbm, values)
     load_weights(2)
-    load("outw", outw_hbm, outw)
+    for step in range(n):
+        target = 2 * lax.rem(spot + (order + [0])[step % half_n], half_n)
+        at = row_columns(target + (1 - pair if step < half_n else pair))
+        load(("outw", step), outw_hbm.at[:, at], outw.at[:, at])
     load("tokens", tokens_hbm, tokens_ref)
     load("dgain", dgain_hbm, dgain_ref)
     load("hgain", hgain_hbm, hgain_ref)
@@ -250,12 +263,6 @@
             send_sem=pair_send.at[phase], recv_sem=pair_recv.at[phase],
             device_id={"section": 1 - sec}, device_id_type=MESH,
         )
-
-    half_n = n // 2
-    pair = lax.rem(me, 2)
-    spot = me // 2
-    mate = 2 * spot + 1 - pair
-    order = sorted(range(1, half_n), key=lambda d: abs(d - half_n // 2))
 
     def halves(size):
         return [(h, slice(h * size // 2, (h + 1) * size // 2)) for h in range(2)]
@@ -373,12 +380,12 @@
     own_weights = jnp.concatenate(own_weights, axis=0)
     mixed = (mixed + own_weights * projected(2)).astype(bf)
 
-    loads["outw"].wait()
-    slim = width // n
+    steps = iter(range(n))
     pl.semaphore_wait(barrier, n)
 
     def row_block(j):
-        return product(mixed, outw[:, pl.ds(pl.multiple_of(j * slim, slim), slim)])
+        loads["outw", next(steps)].wait()
+        return product(mixed, outw[:, row_columns(j)])
 
     summed = summed_over_tp(0, row_block, tbuf)
 
@@ -502,9 +509,9 @@
             self.a = a
             self.copies = []
 
-        def send(self, phase, i, place, peer):
-            there = nrm.at[place, self.a]
-            copy = to_peer(phase, 2 * i + self.a, there, there, peer)
+        def send(self, phase, d, place, at, peer):
+            there = nrm.at[place, self.a, at]
+            copy = to_peer(phase, d, there, there, peer)
             copy.start()
             return copy
 
@@ -512,13 +519,15 @@
             nrm[me, self.a] = (block * dgain_ref[:, features(me)]).astype(bf)
             for i, d in enumerate(order):
                 peer = 2 * lax.rem(spot + d, half_n) + pair
-                self.copies.append(self.send(6, i, me, peer))
-            self.send(7, 0, me, mate)
+                for h, at in halves(nrm.shape[2]):
+                    self.copies.append(self.send(6, 4 * i + 2 * h + self.a, me, at, peer))
+            self.send(7, self.a, me, slice(None), mate)
 
         def forward_one(self, i):
             came = 2 * lax.rem(spot - order[i] + half_n, half_n) + pair
-            self.copies[i].wait_recv()
-            self.send(7, 0, came, mate)
+            for h, at in halves(nrm.shape[2]):
+                self.copies[2 * i + h].wait_recv()
+                self.send(7, self.a, came, at, mate)
 
         def forward(self):
             for i in range(half_n - 1):
@@ -702,9 +711,9 @@
         pltpu.VMEM((2, 2, n, 8, total // 2), f32),
         pltpu.VMEM((2, codes, s_local, lanes), bf),
         pltpu.VMEM((2, total // 2, part), f32),
-        pltpu.SemaphoreType.DMA((3 * pieces + 14,)),
+        pltpu.SemaphoreType.DMA((3 * pieces + 13 + n,)),
         pltpu.SemaphoreType.DMA((14,)),
-        pltpu.SemaphoreType.DMA((7 * n + 4,)),
+        pltpu.SemaphoreType.DMA((8 * n + 2,)),
         pltpu.SemaphoreType.DMA((3,)),
         pltpu.SemaphoreType.DMA((3,)),
     ]

time: 64.8 us -> 63.8 us (0.985)
  Pallas kernels: 64 us -> 63 us
    pallas_call x1, Pallas kernels: 63.3 us -> 62.2 us  [fused(): pl.pallas_call(functools.partial(tick_kernel, n, pieces), out_shape=(pltp...]
where the time goes in v5:
time: 63.8 us; the launch traced here: 63.6 us
  Pallas kernels  63 us (99%)
  between operations  0.64 us (1%)
    pallas_call x1, Pallas kernels, fused(): pl.pallas_call(functools.partial(tick_kernel, n, pieces), out_shape=(pltp...  62.2 us

profile of v5, /device:TPU:0, one launch (start us, length us, event | category | flops | bytes accessed | tf_op | source)
XLA Modules:
  0.0 63.6 jit_solution(2451124261879274396)
XLA Ops:
  0.6 62.2 %shard_map.158 = (bf16[32,512]{1,0:T(8,128)(2,1)S(1)}, f32[4,64,256]{2,1,0:T(8,128)S(1)}) custom-call(bf16[32,4096]{1,0:T(8,128)(2,1)} %hidden_hbm.1, f32[1,4096]{1,0:T(1,128)} %bitcast.5, s32[1,32]{1,0:T(1,128)} %bitcast.9, s32[4,64]{1,0:T(4,128)} %bitcast.8, f32[1,1024]{1,0:T(1,128)} %bitcast.6, f32[1,1024]{1,0:T(1,128)} %bitcast.7, ...), custom_call_target="tpu_custom_call" | custom-call | tf_op jit(solution)/shard_map/pallas_call | solution.py:720
  62.9 0.8 %shard_map.159 = (bf16[32,512]{1,0:T(8,128)(2,1)}, f32[64,4,256]{2,1,0:T(4,128)}) custom-call(bf16[32,512]{1,0:T(8,128)(2,1)S(1)} %get-tuple-element.4.temporal_ref, f32[4,64,256]{2,1,0:T(8,128)S(1)} %get-tuple-element.5.logits_ref), custom_call_target="tpu_custom_call" | custom-call | tf_op jit(solution)/shard_map/pallas_call | solution.py:735
